TPU v7x, 256 devices: a whole 4x4x8 slice. The times are simulated.
256 devices in a mesh: vox: 64 (over z, x, core), chan: 4 (over y).
Axes of the slice: x: 4, y: 4, z: 8, core: 2. Of those that a mesh axis runs over, the one named last changes fastest.
Arguments:
- model_blocks: bfloat16 [23552, 128, 128], P(('vox', 'chan')), may hold values from -0.15625 to 0.15625
- start_image: float32 [2048, 32, 128], P('vox'), may hold values from 0 to 2
- measured: float32 [2048, 32, 128], P(('vox', 'chan')), may hold values from -6 to 6
- step_size: float32 [32], replicated, may hold values from 0.05 to 0.25
- sent_tiles: int32 [64, 64, 4], P('vox'), may hold values from -1 to 31, as said below
- block_rows: int32 [23552], P(('vox', 'chan')), may hold values from 0 to 7
- block_slots: int32 [23552], P(('vox', 'chan')), may hold values from 0 to 255, as said below
Outputs:
- estimate: float32 [2048, 32, 128], P('vox')
- residual: float32 [2048, 32, 128], P(('vox', 'chan'))
Inputs may be any that keep to these rules, and one draw needn't show every extreme that they name: `sent_tiles`: an entry is -1 for an unused slot, else a tile of slab j; the used slots of one pair (j, v) come first, hold distinct tiles, number 1 to 4, and slab v always uses all 4 slots for itself. `block_slots`: every block names a used slot of its own device's vox index v, that is sent_tiles[j, v, s] is not -1.
All inputs are finite; a program needn't handle non-finite values.
Results may differ from a plain program's by a relative error of at most 0.0045.
Values may be sent and summed in bfloat16 or wider, within the bound.
A program may use at most 64 MiB of HBM per device.

v0:
```python
import jax
import jax.numpy as jnp
from jax import lax
from jax.sharding import PartitionSpec as P

ITERATIONS = 4


def shards(model_blocks, start_image, measured, step_size, sent_tiles, block_rows, block_slots):
    vox_count = lax.axis_size("vox")
    send_table = sent_tiles[0]
    capacity = send_table.shape[1]
    tile_count = start_image.shape[0]
    wave_count = start_image.shape[1]
    block_width = start_image.shape[2]
    row_count = measured.shape[0]
    block_count = model_blocks.shape[0]
    row_hot = (block_rows[None, :] == jnp.arange(row_count, dtype=jnp.int32)[:, None]).astype(
        jnp.float32
    )
    slot_hot = (
        block_slots[None, :] == jnp.arange(vox_count * capacity, dtype=jnp.int32)[:, None]
    ).astype(jnp.float32)
    tile_range = jnp.arange(tile_count, dtype=jnp.int32)[:, None]
    return_hot = (send_table.reshape(1, -1) == tile_range).astype(jnp.float32)
    step_gains = step_size[None, :, None]
    estimate = start_image
    residual = measured
    for iteration in range(ITERATIONS):
        rounded = estimate.astype(jnp.bfloat16)
        outgoing = jnp.take(rounded, jnp.maximum(send_table, 0), axis=0)
        arrived = lax.all_to_all(outgoing, "vox", split_axis=0, concat_axis=0, tiled=True)
        flat_tiles = arrived.reshape(vox_count * capacity, wave_count, block_width)
        forward_picked = jnp.take(flat_tiles, block_slots, axis=0)
        products = jnp.einsum(
            "bwv,bsv->bws", forward_picked, model_blocks, preferred_element_type=jnp.float32
        )
        summed = jnp.dot(
            row_hot,
            products.reshape(block_count, wave_count * block_width),
            precision=lax.Precision.HIGHEST,
        )
        residual = measured - summed.reshape(row_count, wave_count, block_width)
        narrow = residual.astype(jnp.bfloat16)
        picked = jnp.take(narrow, block_rows, axis=0)
        adjoint_terms = jnp.einsum(
            "bws,bsv->bwv", picked, model_blocks, preferred_element_type=jnp.float32
        )
        slot_sums = jnp.dot(
            slot_hot,
            adjoint_terms.reshape(block_count, wave_count * block_width),
            precision=lax.Precision.HIGHEST,
        )
        slot_sums = slot_sums.reshape(vox_count, capacity, wave_count, block_width)
        returned = lax.all_to_all(slot_sums, "vox", split_axis=0, concat_axis=0, tiled=True)
        local_sum = jnp.dot(
            return_hot,
            returned.reshape(-1, wave_count * block_width),
            precision=lax.Precision.HIGHEST,
        )
        slab_total = lax.psum(local_sum, "chan")
        estimate = jnp.maximum(
            estimate + step_gains * slab_total.reshape(tile_count, wave_count, block_width), 0.0
        )
    return (estimate, residual)


def solution(mesh):
    in_specs = (
        P(("vox", "chan"), None, None),
        P("vox", None, None),
        P(("vox", "chan"), None, None),
        P(),
        P("vox", None, None),
        P(("vox", "chan")),
        P(("vox", "chan")),
    )
    out_specs = (P("vox", None, None), P(("vox", "chan"), None, None))
    return jax.shard_map(shards, mesh=mesh, in_specs=in_specs, out_specs=out_specs, check_vma=False)
```

profile of v0, /device:TPU:2, one launch (start us, length us, event | category | flops | bytes accessed | tf_op | source)
XLA Modules:
  0.0 964.7 jit_solution(2402718531708179896)
XLA Ops:
  15.1 12.3 %all-to-all-start = ((bf16[64,4,32,128]{3,2,1,0:T(8,128)(2,1)}), bf16[64,4,32,128]{3,2,1,0:T(8,128)(2,1)}, u32[]{:S(2)}, u32[]{:S(2)}) async-start(bf16[64,4,32,128]{3,2,1,0:T(8,128)(2,1)} %broadcast_select_fusion.3), calls=%async_computation | async-start | bytes 4194304 | tf_op jit(solution)/shard_map/all_to_all | solution.py:32
  27.6 51.0 %all-to-all-done = bf16[64,4,32,128]{3,2,1,0:T(8,128)(2,1)} async-done(((bf16[64,4,32,128]{3,2,1,0:T(8,128)(2,1)}), bf16[64,4,32,128]{3,2,1,0:T(8,128)(2,1)}, u32[]{:S(2)}, u32[]{:S(2)}) %all-to-all-start) | async-done | bytes 2097184 | tf_op jit(solution)/shard_map/all_to_all | solution.py:32
  78.6 3.1 gather_fusion.1
  81.8 2.8 fusion.79
  93.4 4.4 copy.71
  97.8 6.2 all-to-all-start.1
  104.3 95.7 %all-to-all-done.1 = f32[64,4,32,128]{3,2,1,0:T(8,128)} async-done(((f32[64,4,32,128]{3,2,1,0:T(8,128)}), f32[64,4,32,128]{3,2,1,0:T(8,128)}, u32[]{:S(2)}, u32[]{:S(2)}) %all-to-all-start.1) | async-done | bytes 4194336 | tf_op jit(solution)/shard_map/all_to_all | solution.py:55
  200.0 5.9 fusion.32
  206.8 44.8 %all-reduce.5.cloned.1.call-done = f32[32,32,128]{2,1,0:T(8,128)} async-done(((f32[32,32,128]{2,1,0:T(8,128)}), f32[32,32,128]{2,1,0:T(8,128)}) %all-reduce.5.cloned.1.call-update) | async-done | bytes 524304 | tf_op jit(solution)/shard_map/psum | solution.py:61
  256.9 61.7 %all_to_all.40 = bf16[64,4,32,128]{3,2,1,0:T(8,128)(2,1)} all-to-all(bf16[64,4,32,128]{3,2,1,0:T(8,128)(2,1)S(1)} %broadcast_select_fusion.2), channel_id=1, replica_groups=mesh['vox'=64,'chan'=4] {'vox'}, dimensions={0} | all-to-all | bytes 4194304 | tf_op jit(solution)/shard_map/all_to_all | solution.py:32
  318.6 3.1 gather_fusion.4
  335.1 101.8 %all_to_all.41 = f32[64,4,32,128]{3,2,1,0:T(8,128)S(1)} all-to-all(f32[64,4,32,128]{3,2,1,0:T(8,128)S(1)} %copy.78), channel_id=1, replica_groups=mesh['vox'=64,'chan'=4] {'vox'}, dimensions={0} | all-to-all | bytes 8388608 | tf_op jit(solution)/shard_map/all_to_all | solution.py:55
  436.9 3.9 fusion.35
  441.8 43.9 %all-reduce.7.cloned.1.call-done = f32[32,32,128]{2,1,0:T(8,128)} async-done(((f32[32,32,128]{2,1,0:T(8,128)}), f32[32,32,128]{2,1,0:T(8,128)}) %all-reduce.7.cloned.1.call-update) | async-done | bytes 524304 | tf_op jit(solution)/shard_map/psum | solution.py:61
  492.0 61.8 %all_to_all.42 = bf16[64,4,32,128]{3,2,1,0:T(8,128)(2,1)} all-to-all(bf16[64,4,32,128]{3,2,1,0:T(8,128)(2,1)S(1)} %broadcast_select_fusion.1), channel_id=1, replica_groups=mesh['vox'=64,'chan'=4] {'vox'}, dimensions={0} | all-to-all | bytes 4194304 | tf_op jit(solution)/shard_map/all_to_all | solution.py:32
  553.8 3.1 gather_fusion.7
  570.3 101.6 %all_to_all.43 = f32[64,4,32,128]{3,2,1,0:T(8,128)S(1)} all-to-all(f32[64,4,32,128]{3,2,1,0:T(8,128)S(1)} %copy.85), channel_id=1, replica_groups=mesh['vox'=64,'chan'=4] {'vox'}, dimensions={0} | all-to-all | bytes 8388608 | tf_op jit(solution)/shard_map/all_to_all | solution.py:55
  671.9 3.9 fusion.38
  676.8 43.9 %all-reduce.9.cloned.1.call-done = f32[32,32,128]{2,1,0:T(8,128)} async-done(((f32[32,32,128]{2,1,0:T(8,128)}), f32[32,32,128]{2,1,0:T(8,128)}) %all-reduce.9.cloned.1.call-update) | async-done | bytes 524304 | tf_op jit(solution)/shard_map/psum | solution.py:61
  726.0 61.9 %all_to_all.44 = bf16[64,4,32,128]{3,2,1,0:T(8,128)(2,1)} all-to-all(bf16[64,4,32,128]{3,2,1,0:T(8,128)(2,1)S(1)} %broadcast_select_fusion), channel_id=1, replica_groups=mesh['vox'=64,'chan'=4] {'vox'}, dimensions={0} | all-to-all | bytes 4194304 | tf_op jit(solution)/shard_map/all_to_all | solution.py:32
  787.9 3.1 gather_fusion.10
  805.0 101.7 %all_to_all.45 = f32[64,4,32,128]{3,2,1,0:T(8,128)S(1)} all-to-all(f32[64,4,32,128]{3,2,1,0:T(8,128)S(1)} %copy.92), channel_id=1, replica_groups=mesh['vox'=64,'chan'=4] {'vox'}, dimensions={0} | all-to-all | bytes 8388608 | tf_op jit(solution)/shard_map/all_to_all | solution.py:55
  906.7 3.9 fusion.41
  913.1 42.3 %all-reduce.11.cloned.1.call-done = f32[32,32,128]{2,1,0:T(8,128)} async-done(((f32[32,32,128]{2,1,0:T(8,128)}), f32[32,32,128]{2,1,0:T(8,128)}) %all-reduce.11.cloned.1.call-update) | async-done | bytes 524304 | tf_op jit(solution)/shard_map/psum | solution.py:61
  (89 shorter events, 82.0 us)
Async XLA Ops:
  7.2 74.6 %copy-start = (bf16[92,128,128]{2,1,0:T(8,128)(2,1)S(1)}, bf16[92,128,128]{2,1,0:T(8,128)(2,1)}, u32[]{:S(2)}) copy-start(bf16[92,128,128]{2,1,0:T(8,128)(2,1)} %param.13) | copy-start | bytes 9043972
  15.1 12.4 %copy-start.4 = (s32[92]{0:T(128)S(1)}, s32[92]{0:T(128)}, u32[]{:S(2)}) copy-start(s32[92]{0:T(128)} %param.19) | copy-start | bytes 1108
  15.1 12.4 %copy-start.6 = (s32[92]{0:T(128)S(1)}, s32[92]{0:T(128)}, u32[]{:S(2)}) copy-start(s32[92]{0:T(128)} %param.18) | copy-start | bytes 1108
  15.1 63.5 %all-to-all-start = ((bf16[64,4,32,128]{3,2,1,0:T(8,128)(2,1)}), bf16[64,4,32,128]{3,2,1,0:T(8,128)(2,1)}, u32[]{:S(2)}, u32[]{:S(2)}) async-start(bf16[64,4,32,128]{3,2,1,0:T(8,128)(2,1)} %broadcast_select_fusion.3), calls=%async_computation | async-start | bytes 4194304 | tf_op jit(solution)/shard_map/all_to_all | solution.py:32
  84.6 0.9 copy-start.2
  97.8 6.2 copy-start.3
  97.8 102.1 %all-to-all-start.1 = ((f32[64,4,32,128]{3,2,1,0:T(8,128)}), f32[64,4,32,128]{3,2,1,0:T(8,128)}, u32[]{:S(2)}, u32[]{:S(2)}) async-start(f32[64,4,32,128]{3,2,1,0:T(8,128)} %copy.71), calls=%async_computation.1 | async-start | bytes 8388608 | tf_op jit(solution)/shard_map/all_to_all | solution.py:55
  104.0 147.6 %all-reduce.5.cloned.1.call-start = ((), (), s32[]{:S(2)}) async-start(), calls=%async_computation.8 | async-start | bytes 1048576 | tf_op jit(solution)/shard_map/psum | solution.py:61
  200.0 51.7 %copy-start.5 = (f32[32]{0:T(128)S(1)}, f32[32]{0:T(128)}, u32[]{:S(2)}) copy-start(f32[32]{0:T(128)} %param.16) | copy-start | bytes 388
  206.8 278.9 %all-reduce.7.cloned.1.call-start = ((), (), s32[]{:S(2)}) async-start(), calls=%async_computation.9 | async-start | bytes 1048576 | tf_op jit(solution)/shard_map/psum | solution.py:61
  441.7 278.9 %all-reduce.9.cloned.1.call-start = ((), (), s32[]{:S(2)}) async-start(), calls=%async_computation.10 | async-start | bytes 1048576 | tf_op jit(solution)/shard_map/psum | solution.py:61
  676.8 278.7 %all-reduce.11.cloned.1.call-start = ((), (), s32[]{:S(2)}) async-start(), calls=%async_computation.11 | async-start | bytes 1048576 | tf_op jit(solution)/shard_map/psum | solution.py:61
  910.6 44.8 %copy-start.1 = (f32[32,32,128]{2,1,0:T(8,128)S(1)}, f32[32,32,128]{2,1,0:T(8,128)}, u32[]{:S(2)}) copy-start(f32[32,32,128]{2,1,0:T(8,128)} %get-tuple-element.14) | copy-start | bytes 1572868
Sparse Core Ops, SparseCore 0:
  206.9 44.6 all-reduce.4
  441.8 43.7 all-reduce.6
  676.9 43.7 all-reduce.8
  911.7 43.7 all-reduce.10
where the time goes:
time: 974 us; the launch traced here: 965 us
  blocking collectives  491 us (50%)
  waiting for transfers between devices  322 us (33%)
  matrix products  54.4 us (6%)
  local copies, waits for them, and re-layouts  46.8 us (5%)
  starting transfers between devices  18.7 us (2%)
  other arithmetic  18.1 us (2%)
  between operations  14.6 us (1%)
    all_to_all x3, blocking collectives, shards(): lax.all_to_all(slot_sums, 'vox', split_axis=0, concat_axis=0, tiled=True)  305 us
    all_to_all x3, blocking collectives, shards(): lax.all_to_all(outgoing, 'vox', split_axis=0, concat_axis=0, tiled=True)  185 us
    psum x4, waiting for transfers between devices, shards(): slab_total = lax.psum(local_sum, 'chan')  175 us
    all_to_all x1, waiting for transfers between devices, shards(): lax.all_to_all(slot_sums, 'vox', split_axis=0, concat_axis=0, tiled=True)  95.7 us
    all_to_all x1, waiting for transfers between devices, shards(): lax.all_to_all(outgoing, 'vox', split_axis=0, concat_axis=0, tiled=True)  51 us
  transfers between devices with their start and end apart: 6, of which 6 were waited for; matrix products, arithmetic and copies ran while one was open for 0% of the time, Pallas kernels for 0%

commit v1 on v0

--- a/solution.py
+++ b/solution.py
@@ -4,6 +4,14 @@
 from jax.sharding import PartitionSpec as P
 
 ITERATIONS = 4
+
+
+def doubling_sum(x, axis):
+    n_dev, total = (lax.axis_size(axis), x)
+    for hop in [1 << k for k in range(n_dev.bit_length() - 1)]:
+        pairs = [(i, i ^ hop) for i in range(n_dev)]
+        total = total + lax.ppermute(total, axis, pairs)
+    return total
 
 
 def shards(model_blocks, start_image, measured, step_size, sent_tiles, block_rows, block_slots):
@@ -58,7 +66,7 @@
             returned.reshape(-1, wave_count * block_width),
             precision=lax.Precision.HIGHEST,
         )
-        slab_total = lax.psum(local_sum, "chan")
+        slab_total = doubling_sum(local_sum, "chan")
         estimate = jnp.maximum(
             estimate + step_gains * slab_total.reshape(tile_count, wave_count, block_width), 0.0
         )

time: 974 us -> 877 us (0.900)
  waiting for transfers between devices: 322 us -> 229 us
  starting transfers between devices: 18.7 us -> 38.4 us
  between operations: 14.6 us -> 1.64 us
    psum x4 -> x0, waiting for transfers between devices: 175 us -> none  [shards(): slab_total = lax.psum(local_sum, 'chan')]
    ppermute x0 -> x8, waiting for transfers between devices: none -> 82.2 us  [doubling_sum(): total = total + lax.ppermute(total, axis, pairs)]
    ppermute x0 -> x8, starting transfers between devices: none -> 19.9 us  [doubling_sum(): total = total + lax.ppermute(total, axis, pairs)]
  transfers between devices with their start and end apart: 6 -> 10, of which waited for: 6 -> 10; matrix products, arithmetic and copies ran while one was open for 0% -> 0% of each run, Pallas kernels for 0% -> 0%
where the time goes in v1:
time: 877 us; the launch traced here: 866 us
  blocking collectives  485 us (55%)
  waiting for transfers between devices  229 us (26%)
  matrix products  53.7 us (6%)
  local copies, waits for them, and re-layouts  44.3 us (5%)
  starting transfers between devices  38.4 us (4%)
  other arithmetic  13.6 us (2%)
    all_to_all x3, blocking collectives, shards(): lax.all_to_all(slot_sums, 'vox', split_axis=0, concat_axis=0, tiled=True)  305 us
    all_to_all x3, blocking collectives, shards(): lax.all_to_all(outgoing, 'vox', split_axis=0, concat_axis=0, tiled=True)  180 us
    all_to_all x1, waiting for transfers between devices, shards(): lax.all_to_all(slot_sums, 'vox', split_axis=0, concat_axis=0, tiled=True)  95.7 us
    ppermute x8, waiting for transfers between devices, doubling_sum(): total = total + lax.ppermute(total, axis, pairs)  82.2 us
    all_to_all x1, waiting for transfers between devices, shards(): lax.all_to_all(outgoing, 'vox', split_axis=0, concat_axis=0, tiled=True)  51 us
    ppermute x8, starting transfers between devices, doubling_sum(): total = total + lax.ppermute(total, axis, pairs)  19.9 us
    dot_general x4, matrix products, shards(): jnp.dot(return_hot, returned.reshape(-1, wave_count * block_width), preci...  17.7 us
  transfers between devices with their start and end apart: 10, of which 10 were waited for; matrix products, arithmetic and copies ran while one was open for 0% of the time, Pallas kernels for 0%

profile of v1, /device:TPU:2, one launch (start us, length us, event | category | flops | bytes accessed | tf_op | source)
XLA Modules:
  0.0 866.1 jit_solution(4559521355233734052)
XLA Ops:
  8.6 12.3 %all-to-all-start = ((bf16[64,4,32,128]{3,2,1,0:T(8,128)(2,1)}), bf16[64,4,32,128]{3,2,1,0:T(8,128)(2,1)}, u32[]{:S(2)}, u32[]{:S(2)}) async-start(bf16[64,4,32,128]{3,2,1,0:T(8,128)(2,1)} %broadcast_select_fusion.3), calls=%async_computation | async-start | bytes 4194304 | tf_op jit(solution)/shard_map/all_to_all | solution.py:40
  21.0 51.0 %all-to-all-done = bf16[64,4,32,128]{3,2,1,0:T(8,128)(2,1)} async-done(((bf16[64,4,32,128]{3,2,1,0:T(8,128)(2,1)}), bf16[64,4,32,128]{3,2,1,0:T(8,128)(2,1)}, u32[]{:S(2)}, u32[]{:S(2)}) %all-to-all-start) | async-done | bytes 2097184 | tf_op jit(solution)/shard_map/all_to_all | solution.py:40
  86.9 4.4 copy.71
  91.3 6.2 all-to-all-start.1
  97.7 95.7 %all-to-all-done.1 = f32[64,4,32,128]{3,2,1,0:T(8,128)} async-done(((f32[64,4,32,128]{3,2,1,0:T(8,128)}), f32[64,4,32,128]{3,2,1,0:T(8,128)}, u32[]{:S(2)}, u32[]{:S(2)}) %all-to-all-start.1) | async-done | bytes 4194336 | tf_op jit(solution)/shard_map/all_to_all | solution.py:63
  193.4 5.9 fusion.9
  201.0 10.0 %collective-permute-done = f32[32,4096]{1,0:T(8,128)S(1)} collective-permute-done((f32[32,4096]{1,0:T(8,128)S(1)}, f32[32,4096]{1,0:T(8,128)S(1)}, u32[]{:S(2)}, u32[]{:S(2)}) %collective-permute-start) | collective-permute-done | bytes 524320 | tf_op jit(solution)/shard_map/ppermute | solution.py:13
  211.1 3.4 collective-permute-start.1
  214.4 10.2 %collective-permute-done.1 = f32[32,4096]{1,0:T(8,128)S(1)} collective-permute-done((f32[32,4096]{1,0:T(8,128)S(1)}, f32[32,4096]{1,0:T(8,128)S(1)}, u32[]{:S(2)}, u32[]{:S(2)}) %collective-permute-start.1) | collective-permute-done | bytes 524320 | tf_op jit(solution)/shard_map/ppermute | solution.py:13
  229.8 60.7 %all_to_all.40 = bf16[64,4,32,128]{3,2,1,0:T(8,128)(2,1)} all-to-all(bf16[64,4,32,128]{3,2,1,0:T(8,128)(2,1)S(1)} %broadcast_select_fusion.2), channel_id=1, replica_groups=mesh['vox'=64,'chan'=4] {'vox'}, dimensions={0} | all-to-all | bytes 4194304 | tf_op jit(solution)/shard_map/all_to_all | solution.py:40
  306.9 101.9 %all_to_all.41 = f32[64,4,32,128]{3,2,1,0:T(8,128)S(1)} all-to-all(f32[64,4,32,128]{3,2,1,0:T(8,128)S(1)} %copy.78), channel_id=1, replica_groups=mesh['vox'=64,'chan'=4] {'vox'}, dimensions={0} | all-to-all | bytes 8388608 | tf_op jit(solution)/shard_map/all_to_all | solution.py:63
  408.8 3.9 fusion.6
  414.4 10.6 %collective-permute-done.2 = f32[32,4096]{1,0:T(8,128)S(1)} collective-permute-done((f32[32,4096]{1,0:T(8,128)S(1)}, f32[32,4096]{1,0:T(8,128)S(1)}, u32[]{:S(2)}, u32[]{:S(2)}) %collective-permute-start.2) | collective-permute-done | bytes 524320 | tf_op jit(solution)/shard_map/ppermute | solution.py:13
  428.3 10.3 %collective-permute-done.3 = f32[32,4096]{1,0:T(8,128)S(1)} collective-permute-done((f32[32,4096]{1,0:T(8,128)S(1)}, f32[32,4096]{1,0:T(8,128)S(1)}, u32[]{:S(2)}, u32[]{:S(2)}) %collective-permute-start.3) | collective-permute-done | bytes 524320 | tf_op jit(solution)/shard_map/ppermute | solution.py:13
  443.8 59.7 %all_to_all.42 = bf16[64,4,32,128]{3,2,1,0:T(8,128)(2,1)} all-to-all(bf16[64,4,32,128]{3,2,1,0:T(8,128)(2,1)S(1)} %broadcast_select_fusion.1), channel_id=1, replica_groups=mesh['vox'=64,'chan'=4] {'vox'}, dimensions={0} | all-to-all | bytes 4194304 | tf_op jit(solution)/shard_map/all_to_all | solution.py:40
  520.0 101.6 %all_to_all.43 = f32[64,4,32,128]{3,2,1,0:T(8,128)S(1)} all-to-all(f32[64,4,32,128]{3,2,1,0:T(8,128)S(1)} %copy.85), channel_id=1, replica_groups=mesh['vox'=64,'chan'=4] {'vox'}, dimensions={0} | all-to-all | bytes 8388608 | tf_op jit(solution)/shard_map/all_to_all | solution.py:63
  621.6 3.9 fusion.3
  627.2 10.6 %collective-permute-done.4 = f32[32,4096]{1,0:T(8,128)S(1)} collective-permute-done((f32[32,4096]{1,0:T(8,128)S(1)}, f32[32,4096]{1,0:T(8,128)S(1)}, u32[]{:S(2)}, u32[]{:S(2)}) %collective-permute-start.4) | collective-permute-done | bytes 524320 | tf_op jit(solution)/shard_map/ppermute | solution.py:13
  641.1 10.3 %collective-permute-done.5 = f32[32,4096]{1,0:T(8,128)S(1)} collective-permute-done((f32[32,4096]{1,0:T(8,128)S(1)}, f32[32,4096]{1,0:T(8,128)S(1)}, u32[]{:S(2)}, u32[]{:S(2)}) %collective-permute-start.5) | collective-permute-done | bytes 524320 | tf_op jit(solution)/shard_map/ppermute | solution.py:13
  656.6 59.8 %all_to_all.44 = bf16[64,4,32,128]{3,2,1,0:T(8,128)(2,1)} all-to-all(bf16[64,4,32,128]{3,2,1,0:T(8,128)(2,1)S(1)} %broadcast_select_fusion), channel_id=1, replica_groups=mesh['vox'=64,'chan'=4] {'vox'}, dimensions={0} | all-to-all | bytes 4194304 | tf_op jit(solution)/shard_map/all_to_all | solution.py:40
  732.8 101.7 %all_to_all.45 = f32[64,4,32,128]{3,2,1,0:T(8,128)S(1)} all-to-all(f32[64,4,32,128]{3,2,1,0:T(8,128)S(1)} %copy.92), channel_id=1, replica_groups=mesh['vox'=64,'chan'=4] {'vox'}, dimensions={0} | all-to-all | bytes 8388608 | tf_op jit(solution)/shard_map/all_to_all | solution.py:63
  834.5 3.9 fusion
  840.1 10.6 %collective-permute-done.6 = f32[32,4096]{1,0:T(8,128)S(1)} collective-permute-done((f32[32,4096]{1,0:T(8,128)S(1)}, f32[32,4096]{1,0:T(8,128)S(1)}, u32[]{:S(2)}, u32[]{:S(2)}) %collective-permute-start.6) | collective-permute-done | bytes 524320 | tf_op jit(solution)/shard_map/ppermute | solution.py:13
  854.7 9.7 %collective-permute-done.7 = f32[32,4096]{1,0:T(8,128)S(1)} collective-permute-done((f32[32,4096]{1,0:T(8,128)S(1)}, f32[32,4096]{1,0:T(8,128)S(1)}, u32[]{:S(2)}, u32[]{:S(2)}) %collective-permute-start.7) | collective-permute-done | bytes 524320 | tf_op jit(solution)/shard_map/ppermute | solution.py:13
  (115 shorter events, 106.0 us)
Async XLA Ops:
  0.6 74.6 %copy-start = (bf16[92,128,128]{2,1,0:T(8,128)(2,1)S(1)}, bf16[92,128,128]{2,1,0:T(8,128)(2,1)}, u32[]{:S(2)}) copy-start(bf16[92,128,128]{2,1,0:T(8,128)(2,1)} %param.13) | copy-start | bytes 9043972
  8.6 12.4 %copy-start.11 = (s32[92]{0:T(128)S(1)}, s32[92]{0:T(128)}, u32[]{:S(2)}) copy-start(s32[92]{0:T(128)} %param.19) | copy-start | bytes 1108
  8.6 12.4 %copy-start.13 = (s32[92]{0:T(128)S(1)}, s32[92]{0:T(128)}, u32[]{:S(2)}) copy-start(s32[92]{0:T(128)} %param.18) | copy-start | bytes 1108
  8.6 63.5 %all-to-all-start = ((bf16[64,4,32,128]{3,2,1,0:T(8,128)(2,1)}), bf16[64,4,32,128]{3,2,1,0:T(8,128)(2,1)}, u32[]{:S(2)}, u32[]{:S(2)}) async-start(bf16[64,4,32,128]{3,2,1,0:T(8,128)(2,1)} %broadcast_select_fusion.3), calls=%async_computation | async-start | bytes 4194304 | tf_op jit(solution)/shard_map/all_to_all | solution.py:40
  78.1 0.9 copy-start.9
  91.3 6.2 copy-start.10
  91.3 102.1 %all-to-all-start.1 = ((f32[64,4,32,128]{3,2,1,0:T(8,128)}), f32[64,4,32,128]{3,2,1,0:T(8,128)}, u32[]{:S(2)}, u32[]{:S(2)}) async-start(f32[64,4,32,128]{3,2,1,0:T(8,128)} %copy.71), calls=%async_computation.1 | async-start | bytes 8388608 | tf_op jit(solution)/shard_map/all_to_all | solution.py:63
  199.3 26.3 %copy-start.3 = (f32[32,32,128]{2,1,0:T(8,128)S(1)}, f32[32,32,128]{2,1,0:T(8,128)}, u32[]{:S(2)}) copy-start(f32[32,32,128]{2,1,0:T(8,128)} %param.14) | copy-start | bytes 1572868
  199.3 26.3 %copy-start.12 = (f32[32]{0:T(128)S(1)}, f32[32]{0:T(128)}, u32[]{:S(2)}) copy-start(f32[32]{0:T(128)} %param.16) | copy-start | bytes 388
  199.3 11.6 %collective-permute-start = (f32[32,4096]{1,0:T(8,128)S(1)}, f32[32,4096]{1,0:T(8,128)S(1)}, u32[]{:S(2)}, u32[]{:S(2)}) collective-permute-start(f32[32,4096]{1,0:T(8,128)S(1)} %fusion.9), channel_id=1, source_target_pairs={{0,1},{1,0},{2,3},{3,2},{4,5},{5,4},{6,7},{7,6},{8,9},{9,8},{10,11... | collective-permute-start | bytes 1572872 | tf_op jit(solution)/shard_map/ppermute | solution.py:13
  211.1 13.6 %collective-permute-start.1 = (f32[32,4096]{1,0:T(8,128)S(1)}, f32[32,4096]{1,0:T(8,128)S(1)}, u32[]{:S(2)}, u32[]{:S(2)}) collective-permute-start(f32[32,4096]{1,0:T(8,128)S(1)} %add.61), channel_id=1, source_target_pairs={{0,2},{1,3},{2,0},{3,1},{4,6},{5,7},{6,4},{7,5},{8,10},{9,11},{10,... | collective-permute-start | bytes 1572872 | tf_op jit(solution)/shard_map/ppermute | solution.py:13
  224.8 0.8 copy-start.7
  412.7 26.1 %copy-start.4 = (f32[32,32,128]{2,1,0:T(8,128)S(1)}, f32[32,32,128]{2,1,0:T(8,128)}, u32[]{:S(2)}) copy-start(f32[32,32,128]{2,1,0:T(8,128)} %param.14) | copy-start | bytes 1572868
  412.7 26.1 %copy-start.8 = (f32[4,8,32,128]{3,2,1,0:T(8,128)S(1)}, f32[4,8,32,128]{3,2,1,0:T(8,128)}, u32[]{:S(2)}) copy-start(f32[4,8,32,128]{3,2,1,0:T(8,128)} %copy-done.7) | copy-start | bytes 1572868
  412.7 12.2 %collective-permute-start.2 = (f32[32,4096]{1,0:T(8,128)S(1)}, f32[32,4096]{1,0:T(8,128)S(1)}, u32[]{:S(2)}, u32[]{:S(2)}) collective-permute-start(f32[32,4096]{1,0:T(8,128)S(1)} %fusion.6), channel_id=1, source_target_pairs={{0,1},{1,0},{2,3},{3,2},{4,5},{5,4},{6,7},{7,6},{8,9},{9,8},{10,11... | collective-permute-start | bytes 1572872 | tf_op jit(solution)/shard_map/ppermute | solution.py:13
  425.0 13.6 %collective-permute-start.3 = (f32[32,4096]{1,0:T(8,128)S(1)}, f32[32,4096]{1,0:T(8,128)S(1)}, u32[]{:S(2)}, u32[]{:S(2)}) collective-permute-start(f32[32,4096]{1,0:T(8,128)S(1)} %add.64), channel_id=1, source_target_pairs={{0,2},{1,3},{2,0},{3,1},{4,6},{5,7},{6,4},{7,5},{8,10},{9,11},{10,... | collective-permute-start | bytes 1572872 | tf_op jit(solution)/shard_map/ppermute | solution.py:13
  625.5 26.9 %copy-start.1 = (f32[32,32,128]{2,1,0:T(8,128)S(1)}, f32[32,32,128]{2,1,0:T(8,128)}, u32[]{:S(2)}) copy-start(f32[32,32,128]{2,1,0:T(8,128)} %get-tuple-element.14) | copy-start | bytes 1572868
  625.6 12.2 %collective-permute-start.4 = (f32[32,4096]{1,0:T(8,128)S(1)}, f32[32,4096]{1,0:T(8,128)S(1)}, u32[]{:S(2)}, u32[]{:S(2)}) collective-permute-start(f32[32,4096]{1,0:T(8,128)S(1)} %fusion.3), channel_id=1, source_target_pairs={{0,1},{1,0},{2,3},{3,2},{4,5},{5,4},{6,7},{7,6},{8,9},{9,8},{10,11... | collective-permute-start | bytes 1572872 | tf_op jit(solution)/shard_map/ppermute | solution.py:13
  637.9 13.6 %collective-permute-start.5 = (f32[32,4096]{1,0:T(8,128)S(1)}, f32[32,4096]{1,0:T(8,128)S(1)}, u32[]{:S(2)}, u32[]{:S(2)}) collective-permute-start(f32[32,4096]{1,0:T(8,128)S(1)} %add.67), channel_id=1, source_target_pairs={{0,2},{1,3},{2,0},{3,1},{4,6},{5,7},{6,4},{7,5},{8,10},{9,11},{10,... | collective-permute-start | bytes 1572872 | tf_op jit(solution)/shard_map/ppermute | solution.py:13
  651.6 0.8 copy-start.5
  838.5 26.1 %copy-start.2 = (f32[32,32,128]{2,1,0:T(8,128)S(1)}, f32[32,32,128]{2,1,0:T(8,128)}, u32[]{:S(2)}) copy-start(f32[32,32,128]{2,1,0:T(8,128)} %get-tuple-element.14) | copy-start | bytes 1572868
  838.5 26.1 %copy-start.6 = (f32[4,8,32,128]{3,2,1,0:T(8,128)S(1)}, f32[4,8,32,128]{3,2,1,0:T(8,128)}, u32[]{:S(2)}) copy-start(f32[4,8,32,128]{3,2,1,0:T(8,128)} %copy-done.5) | copy-start | bytes 1572868
  838.5 12.2 %collective-permute-start.6 = (f32[32,4096]{1,0:T(8,128)S(1)}, f32[32,4096]{1,0:T(8,128)S(1)}, u32[]{:S(2)}, u32[]{:S(2)}) collective-permute-start(f32[32,4096]{1,0:T(8,128)S(1)} %fusion), channel_id=1, source_target_pairs={{0,1},{1,0},{2,3},{3,2},{4,5},{5,4},{6,7},{7,6},{8,9},{9,8},{10,11... | collective-permute-start | bytes 1572872 | tf_op jit(solution)/shard_map/ppermute | solution.py:13
  850.8 13.6 %collective-permute-start.7 = (f32[32,4096]{1,0:T(8,128)S(1)}, f32[32,4096]{1,0:T(8,128)S(1)}, u32[]{:S(2)}, u32[]{:S(2)}) collective-permute-start(f32[32,4096]{1,0:T(8,128)S(1)} %add.70), channel_id=1, source_target_pairs={{0,2},{1,3},{2,0},{3,1},{4,6},{5,7},{6,4},{7,5},{8,10},{9,11},{10,... | collective-permute-start | bytes 1572872 | tf_op jit(solution)/shard_map/ppermute | solution.py:13
